TPU v7x, 512 devices: a whole 4x4x16 slice. The times are simulated.
512 devices in a mesh: tm: 64 (over z, x), sx: 4 (over y), sy: 2 (over core).
Axes of the slice: x: 4, y: 4, z: 16, core: 2. Of those that a mesh axis runs over, the one named last changes fastest.
Arguments:
- sources: float32 [128, 32, 32, 128], P('tm', 'sx', 'sy'), may hold values from -6 to 6
- forward_states: float32 [128, 32, 32, 128], P('tm', 'sx', 'sy'), may hold values from -6 to 6
- terminal: float32 [32, 32, 128], P('sx', 'sy'), may hold values from -6 to 6
- damping: float32 [32, 32, 128], P('sx', 'sy'), may hold values from 0.001 to 0.1
- contact_stiff: float32 [8], replicated, may hold values from 0.001 to 1
- regions: int32 [128, 4, 4], P('tm', 'sx', 'sy'), may hold values from 0 to 7
Outputs:
- adjoint: float32 [128, 32, 32, 128], P('tm', 'sx', 'sy')
- damping_grad: float32 [32, 32, 128], P('sx', 'sy')
Inputs may be any that keep to these rules, and one draw needn't show every extreme that they name: `regions`: region of a block of 8 x 8 columns of cells at a step.
All inputs are finite; a program needn't handle non-finite values.
Results may differ from a plain program's by a relative error of at most 0.0003.
Values sent between devices are 32-bit elements; how exact they have to be, the bound alone decides.
No kernel may reach another device: no remote copies, remote signals or barrier semaphores. Data moves between devices by JAX's collectives and lax.ppermute only.
A program may use at most 64 MiB of HBM per device.

v0:
```python
import jax
import jax.numpy as jnp
from jax import lax
from jax.sharding import PartitionSpec as P

SWEEPS = 4
REGIONS = 8
BLOCK_CELLS = 8
coupling = 0.5


def with_halo(array, sides, width):
    for axis, dim in sides:
        count, length = (lax.axis_size(axis), array.shape[dim])
        up = [(i, (i + 1) % count) for i in range(count - 1)]
        down = [(j, i) for i, j in up]
        last = lax.slice_in_dim(array, length - width, length, axis=dim)
        leading = lax.slice_in_dim(array, 0, width, axis=dim)
        before = lax.ppermute(last, axis, up)
        after = lax.ppermute(leading, axis, down)
        array = jnp.concatenate([before, array, after], axis=dim)
    return array


def passed_along(value, axis, steps):
    count = lax.axis_size(axis)
    leading, last = (max(0, -steps), min(count, count - steps))
    return lax.ppermute(value, axis, [(source, source + steps) for source in range(leading, last)])


def neighbours(field):
    extended = with_halo(field, (("sx", 0), ("sy", 1)), 1)
    padded = jnp.pad(extended, ((0, 0), (0, 0), (1, 1)))
    total = padded[2:, 1:-1, 1:-1] + padded[:-2, 1:-1, 1:-1]
    total = total + padded[1:-1, 2:, 1:-1] + padded[1:-1, :-2, 1:-1]
    total = total + padded[1:-1, 1:-1, 2:] + padded[1:-1, 1:-1, :-2]
    return total


def propagate(right, diagonal):
    field = right
    for sweep_index in range(SWEEPS):
        field = (right + coupling * neighbours(field)) / diagonal
    return field


def reaction(region_ids, contact_stiff, damping):
    labels = jnp.arange(REGIONS, dtype=jnp.int32)
    picked = jnp.sum(
        jnp.where(region_ids[:, :, None] == labels, contact_stiff, jnp.zeros_like(contact_stiff)),
        axis=2,
    )
    spread = jnp.repeat(jnp.repeat(picked, BLOCK_CELLS, axis=0), BLOCK_CELLS, axis=1)
    return spread[:, :, None] + damping


def shards(sources, forward_states, terminal, damping, contact_stiff, regions):
    steps_here = sources.shape[0]
    slab_index = lax.axis_index("tm")
    last_slab = slab_index == lax.axis_size("tm") - 1
    zeros_field = jnp.zeros_like(terminal)
    reactions = [
        reaction(regions[position], contact_stiff, damping) for position in range(steps_here)
    ]
    diagonals = [1.0 + reactions[position] + 6.0 * coupling for position in range(steps_here)]
    field = jnp.where(last_slab, terminal, zeros_field)
    for position in range(steps_here - 1, -1, -1):
        field = propagate(field, diagonals[position]) + sources[position]
    coarse_rhs = field
    factor = 1.0 / (1.0 + steps_here * reactions[0])

    def advance(iteration, value):
        return factor * passed_along(value, "tm", -1) + coarse_rhs

    corrected = lax.fori_loop(0, lax.axis_size("tm") - 1, advance, coarse_rhs)
    incoming = passed_along(corrected, "tm", -1)
    field = jnp.where(last_slab, terminal, incoming)
    layers = [corrected] * steps_here
    position = 1
    field = propagate(field, diagonals[position]) + sources[position]
    layers[position] = field
    adjoint = jnp.stack(layers)
    partial_grad = jnp.sum(adjoint * forward_states, axis=0)
    damping_grad = -lax.psum(partial_grad, "tm")
    return (adjoint, damping_grad)


def solution(mesh):
    in_specs = (
        P("tm", "sx", "sy", None),
        P("tm", "sx", "sy", None),
        P("sx", "sy", None),
        P("sx", "sy", None),
        P(),
        P("tm", "sx", "sy"),
    )
    out_specs = (P("tm", "sx", "sy", None), P("sx", "sy", None))
    return jax.shard_map(shards, mesh=mesh, in_specs=in_specs, out_specs=out_specs, check_vma=False)
```

profile of v0, /device:TPU:8, one launch (start us, length us, event | category | flops | bytes accessed | tf_op | source)
XLA Modules:
  0.0 1050.3 jit_solution(4107775764824397045)
XLA Ops:
  7.3 7.7 collective-permute-start.1
  119.7 539.4 %while.10 = (s32[]{:T(128)}, f32[8,16,128]{2,1,0:T(8,128)S(1)}, f32[8,16,128]{2,1,0:T(8,128)S(1)}, f32[8,16,128]{2,1,0:T(8,128)S(1)}, s32[]{:T(128)}) while((s32[]{:T(128)}, f32[8,16,128]{2,1,0:T(8,128)S(1)}, f32[8,16,128]{2,1,0:T(8,128)S(1)}, f32[8,16,128]{2,1,0:T(8,128)S(1)}, s32[]{:T(128)}) %tuple.50), condition=%wide.region_3.4_spmd, body=%wide.region_2.3_spmd.sunk | while | flops 32770 | bytes 524389 | solution.py:75
  121.0 4.9 collective-permute-done
  145.8 5.4 collective-permute-done
  152.5 5.1 collective-permute-done
  159.0 5.3 collective-permute-done
  165.6 7.5 collective-permute-done
  174.4 7.0 collective-permute-done
  182.8 7.2 collective-permute-done
  191.3 6.9 collective-permute-done
  199.5 7.0 collective-permute-done
  207.8 7.0 collective-permute-done
  216.1 7.5 collective-permute-done
  224.8 7.2 collective-permute-done
  233.3 6.8 collective-permute-done
  241.5 6.7 collective-permute-done
  249.5 7.0 collective-permute-done
  257.8 7.0 collective-permute-done
  266.1 7.0 collective-permute-done
  274.4 7.5 collective-permute-done
  283.3 7.1 collective-permute-done
  291.7 6.9 collective-permute-done
  299.9 6.9 collective-permute-done
  308.2 7.0 collective-permute-done
  316.5 7.0 collective-permute-done
  324.8 7.5 collective-permute-done
  333.7 7.0 collective-permute-done
  342.0 6.9 collective-permute-done
  350.3 6.8 collective-permute-done
  358.4 7.0 collective-permute-done
  366.7 7.0 collective-permute-done
  375.0 7.4 collective-permute-done
  383.6 7.1 collective-permute-done
  392.1 7.0 collective-permute-done
  400.5 6.7 collective-permute-done
  408.5 6.6 collective-permute-done
  416.5 7.0 collective-permute-done
  424.8 7.0 collective-permute-done
  433.1 7.0 collective-permute-done
  441.4 7.7 collective-permute-done
  450.4 8.3 collective-permute-done
  460.0 8.5 collective-permute-done
  469.8 8.2 collective-permute-done
  479.3 7.9 collective-permute-done
  488.5 7.9 collective-permute-done
  497.7 8.5 collective-permute-done
  507.5 7.9 collective-permute-done
  516.8 8.2 collective-permute-done
  526.3 9.0 collective-permute-done
  536.6 7.9 collective-permute-done
  545.8 8.4 collective-permute-done
  555.5 8.2 collective-permute-done
  565.1 8.1 collective-permute-done
  574.5 8.2 collective-permute-done
  584.0 8.6 collective-permute-done
  593.9 8.3 collective-permute-done
  603.5 8.3 collective-permute-done
  613.2 8.3 collective-permute-done
  622.8 7.9 collective-permute-done
  632.1 7.9 collective-permute-done
  641.3 8.5 collective-permute-done
  651.1 7.9 collective-permute-done
  660.3 8.2 collective-permute-done.33
  722.3 319.6 %all-reduce.14.cloned.1.call-done = f32[8,16,128]{2,1,0:T(8,128)} async-done(((f32[8,16,128]{2,1,0:T(8,128)}), f32[8,16,128]{2,1,0:T(8,128)}) %all-reduce.14.cloned.1.call-update) | async-done | bytes 65552 | tf_op jit(solution)/shard_map/psum | solution.py:84
  (298 shorter events, 257.2 us)
Async XLA Ops:
  7.2 1034.8 %all-reduce.14.cloned.1.call-start = ((), (), s32[]{:S(2)}) async-start(), calls=%async_computation | async-start | bytes 131072 | tf_op jit(solution)/shard_map/psum | solution.py:84
  7.3 9.7 collective-permute-start.1
  119.7 6.2 collective-permute-start
  132.1 6.2 collective-permute-start
  144.5 6.7 collective-permute-start
  151.2 6.4 collective-permute-start
  157.7 6.6 collective-permute-start
  164.3 8.8 collective-permute-start
  173.1 8.3 collective-permute-start
  181.5 8.5 collective-permute-start
  190.0 8.2 collective-permute-start
  198.2 8.3 collective-permute-start
  206.5 8.3 collective-permute-start
  214.8 8.8 collective-permute-start
  223.5 8.5 collective-permute-start
  232.0 8.1 collective-permute-start
  240.2 8.0 collective-permute-start
  248.2 8.3 collective-permute-start
  256.5 8.3 collective-permute-start
  264.8 8.3 collective-permute-start
  273.1 8.8 collective-permute-start
  282.0 8.4 collective-permute-start
  290.4 8.2 collective-permute-start
  298.6 8.2 collective-permute-start
  306.9 8.3 collective-permute-start
  315.2 8.3 collective-permute-start
  323.5 8.8 collective-permute-start
  332.4 8.3 collective-permute-start
  340.7 8.2 collective-permute-start
  349.0 8.1 collective-permute-start
  357.1 8.3 collective-permute-start
  365.4 8.3 collective-permute-start
  373.7 8.7 collective-permute-start
  382.3 8.4 collective-permute-start
  390.8 8.3 collective-permute-start
  399.2 8.0 collective-permute-start
  407.2 7.9 collective-permute-start
  415.2 8.3 collective-permute-start
  423.5 8.3 collective-permute-start
  431.8 8.3 collective-permute-start
  440.1 9.0 collective-permute-start
  449.1 9.6 collective-permute-start
  458.7 9.8 collective-permute-start
  468.5 9.5 collective-permute-start
  478.0 9.2 collective-permute-start
  487.2 9.2 collective-permute-start
  496.4 9.8 collective-permute-start
  506.2 9.2 collective-permute-start
  515.5 9.5 collective-permute-start
  525.0 10.3 collective-permute-start
  535.3 9.2 collective-permute-start
  544.5 9.7 collective-permute-start
  554.2 9.5 collective-permute-start
  563.8 9.4 collective-permute-start
  573.2 9.5 collective-permute-start
  582.7 9.9 collective-permute-start
  592.6 9.6 collective-permute-start
  602.2 9.6 collective-permute-start
  611.9 9.6 collective-permute-start
  621.5 9.2 collective-permute-start
  630.8 9.2 collective-permute-start
  640.0 9.8 collective-permute-start
  649.8 9.2 collective-permute-start
  659.0 9.5 collective-permute-start.33
  (55 other events, 263.9 us)
Sparse Core Ops, SparseCore 0:
  722.4 319.4 all-reduce.13
where the time goes:
time: 1050 us
  waiting for transfers between devices  815 us (78%)
  starting transfers between devices  209 us (20%)
  between operations  15 us (1%)
    ppermute x64, waiting for transfers between devices, passed_along(): lax.ppermute(value, axis, [(source, source + steps) for source in range(l...  464 us
    psum x1, waiting for transfers between devices, shards(): damping_grad = -lax.psum(partial_grad, 'tm')  320 us
    ppermute x64, starting transfers between devices, passed_along(): lax.ppermute(value, axis, [(source, source + steps) for source in range(l...  82.7 us
    ppermute x24, starting transfers between devices, with_halo(): before = lax.ppermute(last, axis, up)  81.6 us
    ppermute x24, starting transfers between devices, with_halo(): after = lax.ppermute(leading, axis, down)  44.4 us
    ppermute x24, waiting for transfers between devices, with_halo(): before = lax.ppermute(last, axis, up)  28.2 us
  transfers between devices with their start and end apart: 113, of which 88 were waited for; matrix products, arithmetic and copies ran while one was open for 0% of the time, Pallas kernels for 0%

commit v1 on v0

--- a/solution.py
+++ b/solution.py
@@ -81,7 +81,7 @@
     layers[position] = field
     adjoint = jnp.stack(layers)
     partial_grad = jnp.sum(adjoint * forward_states, axis=0)
-    damping_grad = -lax.psum(partial_grad, "tm")
+    damping_grad = -jnp.sum(lax.all_gather(partial_grad, "tm"), axis=0)
     return (adjoint, damping_grad)
 
 

time: 1050 us -> 934 us (0.89)
  waiting for transfers between devices: 815 us -> 713 us
  starting transfers between devices: 209 us -> 187 us
    psum x1 -> x0, waiting for transfers between devices: 320 us -> none  [shards(): damping_grad = -lax.psum(partial_grad, 'tm')]
    all_gather x0 -> x1, waiting for transfers between devices: none -> 206 us  [shards(): damping_grad = -jnp.sum(lax.all_gather(partial_grad, 'tm'), axis=0)]
    ppermute x24, starting transfers between devices: 81.6 us -> 40.1 us  [with_halo(): before = lax.ppermute(last, axis, up)]
    ppermute x24, waiting for transfers between devices: 3.67 us -> 38.2 us  [with_halo(): after = lax.ppermute(leading, axis, down)]
    ppermute x24, waiting for transfers between devices: 28.2 us -> 0.06 us  [with_halo(): before = lax.ppermute(last, axis, up)]
    ppermute x24, starting transfers between devices: 44.4 us -> 64.1 us  [with_halo(): after = lax.ppermute(leading, axis, down)]
  transfers between devices with their start and end apart: 113 -> 113, of which waited for: 88 -> 89; matrix products, arithmetic and copies ran while one was open for 0% -> 0% of each run, Pallas kernels for 0% -> 0%
where the time goes in v1:
time: 934 us; the launch traced here: 931 us
  waiting for transfers between devices  713 us (76%)
  starting transfers between devices  187 us (20%)
  between operations  14.9 us (2%)
  other arithmetic  12.9 us (1%)
    ppermute x64, waiting for transfers between devices, passed_along(): lax.ppermute(value, axis, [(source, source + steps) for source in range(l...  469 us
    all_gather x1, waiting for transfers between devices, shards(): damping_grad = -jnp.sum(lax.all_gather(partial_grad, 'tm'), axis=0)  206 us
    ppermute x64, starting transfers between devices, passed_along(): lax.ppermute(value, axis, [(source, source + steps) for source in range(l...  82.7 us
    ppermute x24, starting transfers between devices, with_halo(): after = lax.ppermute(leading, axis, down)  64.1 us
    ppermute x24, starting transfers between devices, with_halo(): before = lax.ppermute(last, axis, up)  40.1 us
    ppermute x24, waiting for transfers between devices, with_halo(): after = lax.ppermute(leading, axis, down)  38.2 us
  transfers between devices with their start and end apart: 113, of which 89 were waited for; matrix products, arithmetic and copies ran while one was open for 0% of the time, Pallas kernels for 0%

profile of v1, /device:TPU:8, one launch (start us, length us, event | category | flops | bytes accessed | tf_op | source)
XLA Modules:
  0.0 930.5 jit_solution(2148022377488034591)
XLA Ops:
  10.8 5.5 collective-permute-start.1
  110.8 544.7 %while.10 = (s32[]{:T(128)}, f32[8,16,128]{2,1,0:T(8,128)S(1)}, f32[8,16,128]{2,1,0:T(8,128)S(1)}, f32[8,16,128]{2,1,0:T(8,128)S(1)}, s32[]{:T(128)}) while((s32[]{:T(128)}, f32[8,16,128]{2,1,0:T(8,128)S(1)}, f32[8,16,128]{2,1,0:T(8,128)S(1)}, f32[8,16,128]{2,1,0:T(8,128)S(1)}, s32[]{:T(128)}) %tuple.50), condition=%wide.region_3.4_spmd, body=%wide.region_2.3_spmd.sunk | while | flops 32770 | bytes 524389 | solution.py:75
  130.7 5.0 collective-permute-done
  137.0 7.0 collective-permute-done
  145.3 7.0 collective-permute-done
  153.6 7.4 collective-permute-done
  162.3 7.4 collective-permute-done
  171.1 6.7 collective-permute-done
  179.1 6.7 collective-permute-done
  187.1 7.0 collective-permute-done
  195.4 7.0 collective-permute-done
  203.7 7.0 collective-permute-done
  212.0 7.5 collective-permute-done
  220.8 7.0 collective-permute-done
  229.2 7.2 collective-permute-done
  237.7 6.9 collective-permute-done
  245.9 7.0 collective-permute-done
  254.2 7.0 collective-permute-done
  262.5 7.5 collective-permute-done
  271.3 7.2 collective-permute-done
  279.8 6.8 collective-permute-done
  287.9 6.7 collective-permute-done
  295.9 7.0 collective-permute-done
  304.2 7.0 collective-permute-done
  312.5 7.0 collective-permute-done
  320.8 7.5 collective-permute-done
  329.7 7.1 collective-permute-done
  338.1 7.0 collective-permute-done
  346.4 6.9 collective-permute-done
  354.7 7.0 collective-permute-done
  363.0 7.0 collective-permute-done
  371.3 7.5 collective-permute-done
  380.1 7.0 collective-permute-done
  388.4 7.1 collective-permute-done
  396.8 6.9 collective-permute-done
  405.0 7.0 collective-permute-done
  413.4 6.5 collective-permute-done
  421.3 7.4 collective-permute-done
  430.0 7.0 collective-permute-done
  438.3 6.4 collective-permute-done
  446.0 8.8 collective-permute-done
  456.1 7.9 collective-permute-done
  465.3 8.4 collective-permute-done
  475.1 8.2 collective-permute-done
  484.6 8.1 collective-permute-done
  494.0 8.2 collective-permute-done
  503.5 8.6 collective-permute-done
  513.5 8.3 collective-permute-done
  523.1 8.5 collective-permute-done
  532.9 8.2 collective-permute-done
  542.4 7.9 collective-permute-done
  551.6 7.9 collective-permute-done
  560.8 8.5 collective-permute-done
  570.6 7.9 collective-permute-done
  579.8 8.2 collective-permute-done
  589.4 9.0 collective-permute-done
  599.7 7.9 collective-permute-done
  608.9 8.4 collective-permute-done
  618.6 8.2 collective-permute-done
  628.2 8.1 collective-permute-done
  637.6 8.2 collective-permute-done
  647.1 8.4 collective-permute-done
  656.8 7.9 collective-permute-done.33
  714.7 205.9 %all-gather.3.cloned.1.call-done = f32[512,16,128]{2,1,0:T(8,128)} async-done(((f32[8,16,128]{2,1,0:T(8,128)}), f32[512,16,128]{2,1,0:T(8,128)}) %all-gather.3.cloned.1.call-update) | async-done | bytes 4194320 | tf_op jit(solution)/shard_map/all_gather | solution.py:84
  (295 shorter events, 248.3 us)
Async XLA Ops:
  7.2 913.4 %all-gather.3.cloned.1.call-start = ((), (), s32[]{:S(2)}) async-start(), calls=%async_computation | async-start | bytes 4259840 | tf_op jit(solution)/shard_map/all_gather | solution.py:84
  7.3 9.7 %collective-permute-start.2 = (f32[1,16,128]{2,1,0:T(8,128)S(1)}, f32[1,16,128]{2,1,0:T(8,128)S(1)}, u32[]{:S(2)}, u32[]{:S(2)}) collective-permute-start(f32[1,16,128]{2,1,0:T(8,128)S(1)} %get-tuple-element.85), channel_id=1, source_target_pairs={{0,2},{2,4},{4,6},{1,3},{3,5},{5,7},{8,10},{10,12},{12,14},{9,11},... | collective-permute-start | bytes 24584 | tf_op jit(solution)/shard_map/ppermute | solution.py:19
  10.8 6.9 collective-permute-start.1
  129.4 6.3 collective-permute-start
  135.7 8.3 collective-permute-start
  144.0 8.3 collective-permute-start
  152.3 8.7 collective-permute-start
  161.0 8.7 collective-permute-start
  169.8 8.0 collective-permute-start
  177.8 8.0 collective-permute-start
  185.8 8.3 collective-permute-start
  194.1 8.3 collective-permute-start
  202.4 8.3 collective-permute-start
  210.7 8.8 collective-permute-start
  219.5 8.3 collective-permute-start
  227.9 8.5 collective-permute-start
  236.4 8.2 collective-permute-start
  244.6 8.3 collective-permute-start
  252.9 8.3 collective-permute-start
  261.2 8.8 collective-permute-start
  270.0 8.5 collective-permute-start
  278.5 8.1 collective-permute-start
  286.6 8.0 collective-permute-start
  294.6 8.3 collective-permute-start
  302.9 8.3 collective-permute-start
  311.2 8.3 collective-permute-start
  319.5 8.8 collective-permute-start
  328.4 8.4 collective-permute-start
  336.8 8.3 collective-permute-start
  345.1 8.2 collective-permute-start
  353.4 8.3 collective-permute-start
  361.7 8.3 collective-permute-start
  370.0 8.8 collective-permute-start
  378.8 8.3 collective-permute-start
  387.1 8.4 collective-permute-start
  395.5 8.2 collective-permute-start
  403.7 8.3 collective-permute-start
  412.1 7.8 collective-permute-start
  420.0 8.7 collective-permute-start
  428.7 8.3 collective-permute-start
  437.0 7.7 collective-permute-start
  444.7 10.1 %collective-permute-start = (f32[8,16,128]{2,1,0:T(8,128)S(1)}, f32[8,16,128]{2,1,0:T(8,128)S(1)}, u32[]{:S(2)}, u32[]{:S(2)}) collective-permute-start(f32[8,16,128]{2,1,0:T(8,128)S(1)} %get-tuple-element.120), channel_id=1, source_target_pairs={{8,0},{16,8},{24,16},{32,24},{40,32},{48,40},{56,48},{64,56},{72,6... | collective-permute-start | bytes 196616 | tf_op jit(solution)/shard_map/while/body/eval_jaxpr/ppermute | solution.py:28
  454.8 9.2 collective-permute-start
  464.0 9.7 %collective-permute-start = (f32[8,16,128]{2,1,0:T(8,128)S(1)}, f32[8,16,128]{2,1,0:T(8,128)S(1)}, u32[]{:S(2)}, u32[]{:S(2)}) collective-permute-start(f32[8,16,128]{2,1,0:T(8,128)S(1)} %get-tuple-element.120), channel_id=1, source_target_pairs={{8,0},{16,8},{24,16},{32,24},{40,32},{48,40},{56,48},{64,56},{72,6... | collective-permute-start | bytes 196616 | tf_op jit(solution)/shard_map/while/body/eval_jaxpr/ppermute | solution.py:28
  473.8 9.5 %collective-permute-start = (f32[8,16,128]{2,1,0:T(8,128)S(1)}, f32[8,16,128]{2,1,0:T(8,128)S(1)}, u32[]{:S(2)}, u32[]{:S(2)}) collective-permute-start(f32[8,16,128]{2,1,0:T(8,128)S(1)} %get-tuple-element.120), channel_id=1, source_target_pairs={{8,0},{16,8},{24,16},{32,24},{40,32},{48,40},{56,48},{64,56},{72,6... | collective-permute-start | bytes 196616 | tf_op jit(solution)/shard_map/while/body/eval_jaxpr/ppermute | solution.py:28
  483.3 9.4 %collective-permute-start = (f32[8,16,128]{2,1,0:T(8,128)S(1)}, f32[8,16,128]{2,1,0:T(8,128)S(1)}, u32[]{:S(2)}, u32[]{:S(2)}) collective-permute-start(f32[8,16,128]{2,1,0:T(8,128)S(1)} %get-tuple-element.120), channel_id=1, source_target_pairs={{8,0},{16,8},{24,16},{32,24},{40,32},{48,40},{56,48},{64,56},{72,6... | collective-permute-start | bytes 196616 | tf_op jit(solution)/shard_map/while/body/eval_jaxpr/ppermute | solution.py:28
  492.7 9.5 %collective-permute-start = (f32[8,16,128]{2,1,0:T(8,128)S(1)}, f32[8,16,128]{2,1,0:T(8,128)S(1)}, u32[]{:S(2)}, u32[]{:S(2)}) collective-permute-start(f32[8,16,128]{2,1,0:T(8,128)S(1)} %get-tuple-element.120), channel_id=1, source_target_pairs={{8,0},{16,8},{24,16},{32,24},{40,32},{48,40},{56,48},{64,56},{72,6... | collective-permute-start | bytes 196616 | tf_op jit(solution)/shard_map/while/body/eval_jaxpr/ppermute | solution.py:28
  502.2 9.9 %collective-permute-start = (f32[8,16,128]{2,1,0:T(8,128)S(1)}, f32[8,16,128]{2,1,0:T(8,128)S(1)}, u32[]{:S(2)}, u32[]{:S(2)}) collective-permute-start(f32[8,16,128]{2,1,0:T(8,128)S(1)} %get-tuple-element.120), channel_id=1, source_target_pairs={{8,0},{16,8},{24,16},{32,24},{40,32},{48,40},{56,48},{64,56},{72,6... | collective-permute-start | bytes 196616 | tf_op jit(solution)/shard_map/while/body/eval_jaxpr/ppermute | solution.py:28
  512.2 9.6 %collective-permute-start = (f32[8,16,128]{2,1,0:T(8,128)S(1)}, f32[8,16,128]{2,1,0:T(8,128)S(1)}, u32[]{:S(2)}, u32[]{:S(2)}) collective-permute-start(f32[8,16,128]{2,1,0:T(8,128)S(1)} %get-tuple-element.120), channel_id=1, source_target_pairs={{8,0},{16,8},{24,16},{32,24},{40,32},{48,40},{56,48},{64,56},{72,6... | collective-permute-start | bytes 196616 | tf_op jit(solution)/shard_map/while/body/eval_jaxpr/ppermute | solution.py:28
  521.8 9.8 %collective-permute-start = (f32[8,16,128]{2,1,0:T(8,128)S(1)}, f32[8,16,128]{2,1,0:T(8,128)S(1)}, u32[]{:S(2)}, u32[]{:S(2)}) collective-permute-start(f32[8,16,128]{2,1,0:T(8,128)S(1)} %get-tuple-element.120), channel_id=1, source_target_pairs={{8,0},{16,8},{24,16},{32,24},{40,32},{48,40},{56,48},{64,56},{72,6... | collective-permute-start | bytes 196616 | tf_op jit(solution)/shard_map/while/body/eval_jaxpr/ppermute | solution.py:28
  531.6 9.5 %collective-permute-start = (f32[8,16,128]{2,1,0:T(8,128)S(1)}, f32[8,16,128]{2,1,0:T(8,128)S(1)}, u32[]{:S(2)}, u32[]{:S(2)}) collective-permute-start(f32[8,16,128]{2,1,0:T(8,128)S(1)} %get-tuple-element.120), channel_id=1, source_target_pairs={{8,0},{16,8},{24,16},{32,24},{40,32},{48,40},{56,48},{64,56},{72,6... | collective-permute-start | bytes 196616 | tf_op jit(solution)/shard_map/while/body/eval_jaxpr/ppermute | solution.py:28
  541.1 9.2 collective-permute-start
  550.3 9.2 collective-permute-start
  559.5 9.8 %collective-permute-start = (f32[8,16,128]{2,1,0:T(8,128)S(1)}, f32[8,16,128]{2,1,0:T(8,128)S(1)}, u32[]{:S(2)}, u32[]{:S(2)}) collective-permute-start(f32[8,16,128]{2,1,0:T(8,128)S(1)} %get-tuple-element.120), channel_id=1, source_target_pairs={{8,0},{16,8},{24,16},{32,24},{40,32},{48,40},{56,48},{64,56},{72,6... | collective-permute-start | bytes 196616 | tf_op jit(solution)/shard_map/while/body/eval_jaxpr/ppermute | solution.py:28
  569.3 9.2 collective-permute-start
  578.5 9.5 %collective-permute-start = (f32[8,16,128]{2,1,0:T(8,128)S(1)}, f32[8,16,128]{2,1,0:T(8,128)S(1)}, u32[]{:S(2)}, u32[]{:S(2)}) collective-permute-start(f32[8,16,128]{2,1,0:T(8,128)S(1)} %get-tuple-element.120), channel_id=1, source_target_pairs={{8,0},{16,8},{24,16},{32,24},{40,32},{48,40},{56,48},{64,56},{72,6... | collective-permute-start | bytes 196616 | tf_op jit(solution)/shard_map/while/body/eval_jaxpr/ppermute | solution.py:28
  588.1 10.3 %collective-permute-start = (f32[8,16,128]{2,1,0:T(8,128)S(1)}, f32[8,16,128]{2,1,0:T(8,128)S(1)}, u32[]{:S(2)}, u32[]{:S(2)}) collective-permute-start(f32[8,16,128]{2,1,0:T(8,128)S(1)} %get-tuple-element.120), channel_id=1, source_target_pairs={{8,0},{16,8},{24,16},{32,24},{40,32},{48,40},{56,48},{64,56},{72,6... | collective-permute-start | bytes 196616 | tf_op jit(solution)/shard_map/while/body/eval_jaxpr/ppermute | solution.py:28
  598.4 9.2 collective-permute-start
  607.6 9.7 %collective-permute-start = (f32[8,16,128]{2,1,0:T(8,128)S(1)}, f32[8,16,128]{2,1,0:T(8,128)S(1)}, u32[]{:S(2)}, u32[]{:S(2)}) collective-permute-start(f32[8,16,128]{2,1,0:T(8,128)S(1)} %get-tuple-element.120), channel_id=1, source_target_pairs={{8,0},{16,8},{24,16},{32,24},{40,32},{48,40},{56,48},{64,56},{72,6... | collective-permute-start | bytes 196616 | tf_op jit(solution)/shard_map/while/body/eval_jaxpr/ppermute | solution.py:28
  617.3 9.5 %collective-permute-start = (f32[8,16,128]{2,1,0:T(8,128)S(1)}, f32[8,16,128]{2,1,0:T(8,128)S(1)}, u32[]{:S(2)}, u32[]{:S(2)}) collective-permute-start(f32[8,16,128]{2,1,0:T(8,128)S(1)} %get-tuple-element.120), channel_id=1, source_target_pairs={{8,0},{16,8},{24,16},{32,24},{40,32},{48,40},{56,48},{64,56},{72,6... | collective-permute-start | bytes 196616 | tf_op jit(solution)/shard_map/while/body/eval_jaxpr/ppermute | solution.py:28
  626.9 9.4 %collective-permute-start = (f32[8,16,128]{2,1,0:T(8,128)S(1)}, f32[8,16,128]{2,1,0:T(8,128)S(1)}, u32[]{:S(2)}, u32[]{:S(2)}) collective-permute-start(f32[8,16,128]{2,1,0:T(8,128)S(1)} %get-tuple-element.120), channel_id=1, source_target_pairs={{8,0},{16,8},{24,16},{32,24},{40,32},{48,40},{56,48},{64,56},{72,6... | collective-permute-start | bytes 196616 | tf_op jit(solution)/shard_map/while/body/eval_jaxpr/ppermute | solution.py:28
  636.3 9.5 %collective-permute-start = (f32[8,16,128]{2,1,0:T(8,128)S(1)}, f32[8,16,128]{2,1,0:T(8,128)S(1)}, u32[]{:S(2)}, u32[]{:S(2)}) collective-permute-start(f32[8,16,128]{2,1,0:T(8,128)S(1)} %get-tuple-element.120), channel_id=1, source_target_pairs={{8,0},{16,8},{24,16},{32,24},{40,32},{48,40},{56,48},{64,56},{72,6... | collective-permute-start | bytes 196616 | tf_op jit(solution)/shard_map/while/body/eval_jaxpr/ppermute | solution.py:28
  645.8 9.7 %collective-permute-start = (f32[8,16,128]{2,1,0:T(8,128)S(1)}, f32[8,16,128]{2,1,0:T(8,128)S(1)}, u32[]{:S(2)}, u32[]{:S(2)}) collective-permute-start(f32[8,16,128]{2,1,0:T(8,128)S(1)} %get-tuple-element.120), channel_id=1, source_target_pairs={{8,0},{16,8},{24,16},{32,24},{40,32},{48,40},{56,48},{64,56},{72,6... | collective-permute-start | bytes 196616 | tf_op jit(solution)/shard_map/while/body/eval_jaxpr/ppermute | solution.py:28
  655.5 9.2 collective-permute-start.33
  (53 other events, 1665.2 us)
Sparse Core Ops, SparseCore 0:
  714.8 205.7 all-gather.2
